TPU v7x, 32 devices: a whole 2x2x4 slice. The times are simulated.
32 devices in a mesh: prow: 8 (over y, x, core), pcol: 4 (over z).
Axes of the slice: x: 2, y: 2, z: 4, core: 2. Of those that a mesh axis runs over, the one named last changes fastest.
Arguments:
- inverse: bfloat16 [4, 4096, 8, 2048], P(None, 'prow', None, 'pcol'), may hold values from -6 to 6
- panel: bfloat16 [2, 4, 4096, 256], P(None, None, 'prow'), may hold values from -0.09375 to 0.09375
- structure: int32 [2, 8], replicated, may hold values from 0 to 31, as said below
- diag_inverse: float32 [2, 256, 256], replicated, may hold values from -6 to 6
Outputs:
- off_diag: bfloat16 [2, 4, 4096, 256], P(None, None, ('prow', 'pcol'))
- diag_block: float32 [2, 256, 256], replicated
Inputs may be any that keep to these rules, and one draw needn't show every extreme that they name: `structure`: each row lists 8 distinct block indices in increasing order, exactly one of them congruent to p modulo 8 for every p, and always includes the last ancestor block 31.
All inputs are finite; a program needn't handle non-finite values.
Results may differ from a plain program's by a relative error of at most 0.0022.
Values may be sent and summed in bfloat16 or wider, within the bound.
A program may use at most 128 MiB of HBM per device.

v0:
```python
import jax
import jax.numpy as jnp
from jax import lax
from jax.sharding import PartitionSpec as P


def on_device(inverse, panel, structure, diag_inverse):
    prow_count = lax.axis_size("prow")
    pcol_count = lax.axis_size("pcol")
    prow_index = lax.axis_index("prow")
    pcol_index = lax.axis_index("pcol")
    rows_local, block_size, cols_local, _ = inverse.shape
    panel_width = panel.shape[3]
    total_blocks = rows_local * prow_count
    piece_rows = block_size // pcol_count
    owner_ratio = prow_count // pcol_count
    repeat_count = cols_local // owner_ratio
    positions = jnp.arange(total_blocks, dtype=jnp.int32)
    local_rows = jnp.arange(rows_local, dtype=jnp.int32)
    pieces = []
    products = []
    for supernode in range(structure.shape[0]):
        chosen = structure[supernode]
        selected = jnp.any(chosen[:, None] == positions[None, :], axis=0)
        own_rows = lax.dynamic_index_in_dim(
            selected.reshape(rows_local, prow_count), prow_index, 1, keepdims=False
        )
        own_cols = lax.dynamic_index_in_dim(
            selected.reshape(cols_local, pcol_count), pcol_index, 1, keepdims=False
        )
        local_panel = panel[supernode]
        row_pick = jnp.sum(jnp.where(own_rows, local_rows, 0))
        single = lax.dynamic_index_in_dim(local_panel, row_pick, 0, keepdims=False)
        gathered = lax.all_gather(single, "prow", axis=0, tiled=True)
        gathered = gathered.reshape(owner_ratio, pcol_count, block_size, panel_width)
        owner_blocks = lax.dynamic_index_in_dim(gathered, pcol_index, 1, keepdims=False)
        tiled = jnp.broadcast_to(
            owner_blocks[None], (repeat_count, owner_ratio, block_size, panel_width)
        )
        tiled = tiled.reshape(cols_local, block_size, panel_width)
        column_panel = tiled * own_cols.astype(jnp.bfloat16)[:, None, None]
        partial_value = jnp.einsum(
            "racb,cbw->raw", inverse, column_panel, preferred_element_type=jnp.float32
        )
        partial_value = -partial_value * own_rows.astype(jnp.float32)[:, None, None]
        summed = lax.psum_scatter(partial_value, "pcol", scatter_dimension=1, tiled=True)
        rounded = summed.astype(jnp.bfloat16)
        pieces.append(rounded)
        factor_rows = lax.dynamic_slice_in_dim(local_panel, pcol_index * piece_rows, piece_rows, 1)
        products.append(
            jnp.einsum("raw,rav->wv", factor_rows, rounded, preferred_element_type=jnp.float32)
        )
    diagonal_terms = lax.psum(jnp.stack(products), ("prow", "pcol"))
    return (jnp.stack(pieces), diag_inverse - diagonal_terms)


def solution(mesh):
    placed = (P(None, "prow", None, "pcol"), P(None, None, "prow", None), P(), P())
    return jax.shard_map(
        on_device,
        mesh=mesh,
        in_specs=placed,
        out_specs=(P(None, None, ("prow", "pcol"), None), P()),
        check_vma=False,
    )
```

profile of v0, /device:TPU:0, one launch (start us, length us, event | category | flops | bytes accessed | tf_op | source)
XLA Modules:
  0.0 307.7 jit_solution(14271025104973207061)
XLA Ops:
  7.2 0.0 all-gather.5.cloned.1.call-start
  7.2 0.8 slice_bitcast_fusion.1
  8.0 0.1 fusion.24
  8.1 0.1 reshape.64
  8.2 0.2 fusion.30
  8.3 0.6 select_reduce_fusion.1
  10.3 1.7 fusion.32
  12.6 0.7 constant_dynamic-slice_fusion.2
  13.3 0.0 all-gather.5.cloned.1.call-update
  13.4 0.0 all-gather.7.cloned.1.call-start
  13.4 0.1 reshape.68
  13.5 0.2 fusion.31
  13.7 0.6 select_reduce_fusion
  16.3 0.7 constant_dynamic-slice_fusion
  17.0 0.0 all-gather.7.cloned.1.call-update
  17.0 0.0 reduce-scatter.3.cloned.1.call-start
  17.1 0.1 reshape.67
  17.2 0.2 fusion.28
  17.3 26.7 %all-gather.5.cloned.1.call-done = bf16[1,1,4096,256]{3,2,1,0:T(8,128)(2,1)} async-done(((bf16[1,1,512,256]{3,2,1,0:T(8,128)(2,1)}), bf16[1,1,4096,256]{3,2,1,0:T(8,128)(2,1)}) %all-gather.5.cloned.1.call-update) | async-done | bytes 2097168 | tf_op jit(solution)/shard_map/all_gather | solution.py:34
  44.0 1.1 dynamic-slice_bitcast_fusion.1
  45.1 0.2 copy.31
  45.3 1.6 bitcast_multiply_fusion.1
  46.9 18.4 %fusion.8 = f32[4,512,256]{1,2,0:T(8,128)} fusion(bf16[4,512,8,512]{3,2,1,0:T(8,128)(2,1)} %param.4, bf16[8,512,256]{1,2,0:T(8,128)(2,1)} %bitcast_multiply_fusion.1, f32[4]{0:T(128)S(1)} %convert_element_type.42), kind=kOutput, calls=%fused_computation.11 | convolution fusion | flops 4296015872 | bytes 20971536 | tf_op jit(solution)/shard_map/racb,cbw->raw/dot_general | solution.py:42
  65.3 0.0 reduce-scatter.3.cloned.1.call-update
  65.3 0.2 reduce-scatter.5.cloned.1.call-start
  65.5 0.1 reshape.71
  65.6 0.2 fusion.29
  65.8 8.5 %all-gather.7.cloned.1.call-done = bf16[1,1,4096,256]{3,2,1,0:T(8,128)(2,1)} async-done(((bf16[1,1,512,256]{3,2,1,0:T(8,128)(2,1)}), bf16[1,1,4096,256]{3,2,1,0:T(8,128)(2,1)}) %all-gather.7.cloned.1.call-update) | async-done | bytes 2097168 | tf_op jit(solution)/shard_map/all_gather | solution.py:34
  74.3 1.1 dynamic-slice_bitcast_fusion
  75.4 0.2 copy.33
  75.6 1.6 bitcast_multiply_fusion
  77.2 18.7 %fusion.5 = f32[4,512,256]{1,2,0:T(8,128)} fusion(bf16[4,512,8,512]{3,2,1,0:T(8,128)(2,1)} %param.4, bf16[8,512,256]{1,2,0:T(8,128)(2,1)} %bitcast_multiply_fusion, f32[4]{0:T(128)S(1)} %convert_element_type.46), kind=kOutput, calls=%fused_computation.6 | convolution fusion | flops 4296015872 | bytes 20971536 | tf_op jit(solution)/shard_map/racb,cbw->raw/dot_general | solution.py:42
  95.8 0.0 reduce-scatter.5.cloned.1.call-update
  95.9 0.0 all-reduce.2.cloned.1.call-start
  95.9 24.3 %reduce-scatter.3.cloned.1.call-done = f32[4,128,256]{1,2,0:T(8,128)} async-done(((f32[4,512,256]{1,2,0:T(8,128)}), f32[4,128,256]{1,2,0:T(8,128)}) %reduce-scatter.3.cloned.1.call-update) | async-done | bytes 524304 | tf_op jit(solution)/shard_map/reduce_scatter | solution.py:46
  120.2 0.0 copy-start
  120.3 1.4 convolution_bitcast_fusion.1
  121.6 43.6 %reduce-scatter.5.cloned.1.call-done = f32[4,128,256]{1,2,0:T(8,128)} async-done(((f32[4,512,256]{1,2,0:T(8,128)}), f32[4,128,256]{1,2,0:T(8,128)}) %reduce-scatter.5.cloned.1.call-update) | async-done | bytes 524304 | tf_op jit(solution)/shard_map/reduce_scatter | solution.py:46
  165.3 1.4 convolution_bitcast_fusion
  166.6 0.8 pad_maximum_fusion.1
  167.5 0.0 all-reduce.2.cloned.1.call-update
  167.5 0.0 copy-done
  167.6 0.0 copy-done.1
  167.6 0.1 pad_maximum_fusion
  167.7 1.0 copy.39
  168.7 130.6 %all-reduce.2.cloned.1.call-done = f32[2,256,256]{2,1,0:T(8,128)} async-done(((f32[2,256,256]{2,1,0:T(8,128)}), f32[2,256,256]{2,1,0:T(8,128)}) %all-reduce.2.cloned.1.call-update) | async-done | bytes 524304 | tf_op jit(solution)/shard_map/psum | solution.py:53
  299.2 0.0 copy-done.2
  299.3 1.9 sub.3
  (6 shorter events, 0.1 us)
Async XLA Ops:
  7.2 36.9 %all-gather.5.cloned.1.call-start = ((), (), s32[]{:S(2)}) async-start(), calls=%async_computation.5 | async-start | bytes 2359296 | tf_op jit(solution)/shard_map/all_gather | solution.py:34
  13.4 60.9 %all-gather.7.cloned.1.call-start = ((), (), s32[]{:S(2)}) async-start(), calls=%async_computation.6 | async-start | bytes 2359296 | tf_op jit(solution)/shard_map/all_gather | solution.py:34
  17.0 103.2 %reduce-scatter.3.cloned.1.call-start = ((), (), s32[]{:S(2)}) async-start(), calls=%async_computation.2 | async-start | bytes 2621440 | tf_op jit(solution)/shard_map/reduce_scatter | solution.py:46
  65.3 99.9 %reduce-scatter.5.cloned.1.call-start = ((), (), s32[]{:S(2)}) async-start(), calls=%async_computation.3 | async-start | bytes 2621440 | tf_op jit(solution)/shard_map/reduce_scatter | solution.py:46
  95.9 203.4 %all-reduce.2.cloned.1.call-start = ((), (), s32[]{:S(2)}) async-start(), calls=%async_computation.4 | async-start | bytes 1048576 | tf_op jit(solution)/shard_map/psum | solution.py:53
  120.2 47.3 %copy-start = (f32[4,128,256]{1,2,0:T(8,128)S(1)}, f32[4,128,256]{1,2,0:T(8,128)}, u32[]{:S(2)}) copy-start(f32[4,128,256]{1,2,0:T(8,128)} %reduce-scatter.3.cloned.1.call-done) | copy-start | bytes 1572868
  165.2 2.3 copy-start.1
  167.5 131.8 %copy-start.2 = (f32[2,256,256]{2,1,0:T(8,128)S(1)}, f32[2,256,256]{2,1,0:T(8,128)}, u32[]{:S(2)}) copy-start(f32[2,256,256]{2,1,0:T(8,128)} %param.7) | copy-start | bytes 1572868
Sparse Core Ops, SparseCore 0:
  13.5 30.4 all-gather.4
  46.5 27.7 all-gather.6
  76.6 43.6 reduce-scatter.2
  122.4 42.8 reduce-scatter.4
  170.9 128.2 all-reduce.1
where the time goes:
time: 308 us
  waiting for transfers between devices  234 us (76%)
  matrix products  39.9 us (13%)
  between operations  17.8 us (6%)
  local copies, waits for them, and re-layouts  8.2 us (3%)
  other arithmetic  7.75 us (3%)
    psum x1, waiting for transfers between devices, on_device(): diagonal_terms = lax.psum(jnp.stack(products), ('prow', 'pcol'))  131 us
    reduce_scatter x2, waiting for transfers between devices, on_device(): lax.psum_scatter(partial_value, 'pcol', scatter_dimension=1, tiled=True)  67.9 us
    dot_general x2, matrix products, on_device(): jnp.einsum('racb,cbw->raw', inverse, column_panel, preferred_element_type...  37.1 us
    all_gather x2, waiting for transfers between devices, on_device(): gathered = lax.all_gather(single, 'prow', axis=0, tiled=True)  35.1 us
  transfers between devices with their start and end apart: 5, of which 5 were waited for; matrix products, arithmetic and copies ran while one was open for 15% of the time, Pallas kernels for 0%

commit v1 on v0

v1 whole, which is shorter than its diff:
```python
import functools

import jax
import jax.numpy as jnp
from jax import lax
from jax.experimental import pallas as pl
from jax.experimental.pallas import tpu as pltpu
from jax.sharding import PartitionSpec as P

MESH = pl.DeviceIdType.MESH
CHUNKS = 2


def remote(src, dst, send, recv, p, q):
    return pltpu.make_async_remote_copy(
        src_ref=src, dst_ref=dst, send_sem=send, recv_sem=recv, device_id=(p, q), device_id_type=MESH
    )


def fused(
    n_rows, n_cols, a_ref, l_ref, d_ref, y_ref, g_ref,
    l_buf, part, right_buf, left_buf, term, plane_buf, col_buf, gath,
    l_send, l_recv, r_send, r_recv, f_send, f_recv, p_send, p_recv, c_send, c_recv, g_send, g_recv,
):
    p = lax.axis_index("prow")
    q = lax.axis_index("pcol")
    nodes, ratio, block, width = l_buf.shape
    piece = block // n_cols
    seg = width // n_rows
    chunk = block // CHUNKS
    hi = p // n_cols
    lo = p % n_cols
    t = jnp.int32(0)
    bit = 1
    while bit < n_cols:
        t = t + bit * (((lo // bit) + (q // bit)) % 2)
        bit *= 2
    pair = p + 1 - 2 * (p % 2)

    def same_hi(t2):
        lo2 = jnp.int32(0)
        b = 1
        while b < n_cols:
            lo2 = lo2 + b * (((t2 // b) + (q // b)) % 2)
            b *= 2
        return hi * n_cols + lo2

    barrier = pltpu.get_barrier_semaphore()
    for k in range(1, n_rows):
        pl.semaphore_signal(barrier, inc=1, device_id=((p + k) % n_rows, q), device_id_type=MESH)
    for k in range(1, n_cols):
        pl.semaphore_signal(barrier, inc=1, device_id=(p, (q + k) % n_cols), device_id_type=MESH)
    pl.semaphore_wait(barrier, n_rows + n_cols - 2)

    def rows(c):
        return pl.ds(c * chunk, chunk)

    def l_slot(s, h, c):
        return l_buf.at[s, h, rows(c)]

    def to_peer_hi(s, c, k, src):
        return remote(src, l_slot(s, hi, c), l_send.at[s, c, k - 1], l_recv.at[s, hi, c],
                      (p + k * n_cols) % n_rows, q)

    def to_x(s, c, j, src):
        return remote(src, l_slot(s, hi, c), l_send.at[s, c, ratio - 1 + j - 1], l_recv.at[s, hi, c],
                      same_hi(2 * j), q)

    def to_pair(s, c, k, src):
        h = (hi + k) % ratio
        return remote(src, l_slot(s, h, c), l_send.at[s, c, ratio - 1 + n_cols // 2 - 1 + k],
                      l_recv.at[s, h, c], pair, q)

    def l_arrived(s, c, h):
        remote(l_slot(s, h, c), l_slot(s, h, c), l_send.at[s, c, 0], l_recv.at[s, h, c], pair, q).wait_recv()

    owner = t == 0
    even = t % 2 == 0

    @pl.when(owner)
    def _():
        for s in range(nodes):
            for c in range(CHUNKS):
                src = l_ref.at[s, rows(c)]
                for j in range(1, n_cols // 2):
                    to_x(s, c, j, src).start()
                for k in range(1, ratio):
                    to_peer_hi(s, c, k, src).start()
                to_pair(s, c, 0, src).start()
        for s in range(nodes):
            l_buf[s, hi] = l_ref[s]

    def receive_blocks(s):
        for c in range(CHUNKS):
            @pl.when(jnp.logical_not(owner))
            def _():
                l_arrived(s, c, hi)

            @pl.when(jnp.logical_and(even, jnp.logical_not(owner)))
            def _():
                for k in range(1, ratio):
                    to_peer_hi(s, c, k, l_slot(s, hi, c)).start()
                to_pair(s, c, 0, l_slot(s, hi, c)).start()

            for k in range(1, ratio):
                l_arrived(s, c, (hi + k) % ratio)

                @pl.when(even)
                def _():
                    to_pair(s, c, k, l_slot(s, (hi + k) % ratio, c)).start()

    def drain_blocks(s):
        for c in range(CHUNKS):
            @pl.when(even)
            def _():
                src = l_slot(s, hi, c)
                for k in range(1, ratio):
                    to_peer_hi(s, c, k, src).wait_send()
                for k in range(ratio):
                    to_pair(s, c, k, src).wait_send()

            @pl.when(owner)
            def _():
                for j in range(1, n_cols // 2):
                    to_x(s, c, j, l_slot(s, hi, c)).wait_send()

    def multiply(s):
        total = jnp.dot(a_ref[s, 0], l_buf[s, 0], preferred_element_type=jnp.float32)
        for h in range(1, ratio):
            total += jnp.dot(a_ref[s, h], l_buf[s, h], preferred_element_type=jnp.float32)
        for d in range(n_cols):
            part[s, d] = total[d * piece:(d + 1) * piece]

    def right_copy(s, d, src):
        return remote(src, right_buf.at[s, d], r_send.at[s, d], r_recv.at[s, d], p, (q + 1) % n_cols)

    def left_copy(s, d, src):
        return remote(src, left_buf.at[s, d], f_send.at[s, d], f_recv.at[s, d], p, (q + n_cols - 1) % n_cols)

    def line_start(s):
        @pl.when(q == 0)
        def _():
            for d in range(n_cols - 1, 0, -1):
                right_copy(s, d, part.at[s, d]).start()

        @pl.when(q == n_cols - 1)
        def _():
            for d in range(n_cols - 1):
                left_copy(s, d, part.at[s, d]).start()

    def line_relay(s):
        for i in range(n_cols - 2):
            d = n_cols - 1 - i

            @pl.when(jnp.logical_and(q > 0, q < d))
            def _():
                right_copy(s, d, right_buf.at[s, d]).wait_recv()
                right_buf[s, d] = right_buf[s, d] + part[s, d]
                right_copy(s, d, right_buf.at[s, d]).start()

            e = i

            @pl.when(jnp.logical_and(q < n_cols - 1, q > e))
            def _():
                left_copy(s, e, left_buf.at[s, e]).wait_recv()
                left_buf[s, e] = left_buf[s, e] + part[s, e]
                left_copy(s, e, left_buf.at[s, e]).start()

    def line_finish(s):
        @pl.when(q > 0)
        def _():
            right_copy(s, q, right_buf.at[s, q]).wait_recv()
            part[s, q] = part[s, q] + right_buf[s, q]

        @pl.when(q < n_cols - 1)
        def _():
            left_copy(s, q, left_buf.at[s, q]).wait_recv()
            part[s, q] = part[s, q] + left_buf[s, q]

        rounded = (-part[s, q]).astype(jnp.bfloat16)
        y_ref[s] = rounded
        factor = l_ref[s, pl.ds(pl.multiple_of(q * piece, piece), piece)]
        product = lax.dot_general(
            factor, rounded, (((0,), (0,)), ((), ())), preferred_element_type=jnp.float32
        )
        for k in range(n_rows):
            term[s, k] = product[k * seg:(k + 1) * seg]

    def line_drain(s):
        for d in range(n_cols):
            @pl.when(q < d)
            def _():
                right_copy(s, d, part.at[s, d]).wait_send()

            @pl.when(q > d)
            def _():
                left_copy(s, d, part.at[s, d]).wait_send()

    def plane_copy(s, k):
        to = (p + k) % n_rows
        return remote(term.at[s, to], plane_buf.at[s, n_rows - k], p_send.at[s, k], p_recv.at[s, n_rows - k], to, q)

    def plane_wait(s, k):
        remote(term.at[s, 0], plane_buf.at[s, k], p_send.at[s, k], p_recv.at[s, k], pair, q).wait_recv()

    def col_copy(s, k):
        to = (q + k) % n_cols
        return remote(col_buf.at[s, q], col_buf.at[s, q], c_send.at[s, k], c_recv.at[s, n_cols - k], p, to)

    def col_wait(s, k):
        src = (q + k) % n_cols
        remote(col_buf.at[s, src], col_buf.at[s, src], c_send.at[s, k], c_recv.at[s, k], pair, q).wait_recv()

    def gath_copy(s, k):
        to = (p + k) % n_rows
        return remote(gath.at[s, p], gath.at[s, p], g_send.at[s, k], g_recv.at[s, n_rows - k], to, q)

    def gath_wait(s, k):
        src = (p + k) % n_rows
        remote(gath.at[s, src], gath.at[s, src], g_send.at[s, k], g_recv.at[s, k], pair, q).wait_recv()

    def plane_start(s):
        for k in range(1, n_rows):
            plane_copy(s, k).start()

    def col_start(s):
        total = term[s, p]
        for k in range(1, n_rows):
            plane_wait(s, k)
            total = total + plane_buf[s, k]
        col_buf[s, q] = total
        for k in range(1, n_cols):
            col_copy(s, k).start()

    def gath_start(s):
        for k in range(1, n_cols):
            col_wait(s, k)
        total = col_buf[s, 0]
        for k in range(1, n_cols):
            total = total + col_buf[s, k]
        gath[s, p] = d_ref[s, pl.ds(pl.multiple_of(p * seg, seg), seg)] - total
        for k in range(1, n_rows):
            gath_copy(s, k).start()

    for s in range(nodes):
        receive_blocks(s)
        multiply(s)
        line_start(s)
    for s in range(nodes):
        line_relay(s)
        line_finish(s)
        plane_start(s)
    for s in range(nodes):
        col_start(s)
    for s in range(nodes):
        gath_start(s)
    for s in range(nodes):
        drain_blocks(s)
        line_drain(s)
        for k in range(1, n_rows):
            plane_copy(s, k).wait_send()
        for k in range(1, n_cols):
            col_copy(s, k).wait_send()
    for s in range(nodes):
        for k in range(1, n_rows):
            gath_wait(s, k)
        for k in range(n_rows):
            g_ref[s, k * seg:(k + 1) * seg] = gath[s, k]
    for s in range(nodes):
        for k in range(1, n_rows):
            gath_copy(s, k).wait_send()


def on_device(inverse, panel, structure, diag_inverse):
    n_rows = lax.axis_size("prow")
    n_cols = lax.axis_size("pcol")
    p = lax.axis_index("prow")
    q = lax.axis_index("pcol")
    rows_local, block, cols_local, _ = inverse.shape
    nodes, _, _, width = panel.shape
    ratio = n_rows // n_cols
    piece = block // n_cols
    seg = width // n_rows

    picked_a = []
    picked_l = []
    row_picks = []
    for s in range(nodes):
        chosen = structure[s]
        row = jnp.sum(jnp.where(chosen % n_rows == p, chosen // n_rows, 0))
        row_picks.append(row)
        picked_l.append(lax.dynamic_slice(panel, (s, row, 0, 0), (1, 1, block, width))[0, 0])
        for h in range(ratio):
            col = jnp.sum(jnp.where(chosen % n_rows == h * n_cols + q, chosen // n_cols, 0))
            picked_a.append(
                lax.dynamic_slice(inverse, (row, 0, col, 0), (1, block, 1, block))[0, :, 0, :]
            )
    a_sel = jnp.stack(picked_a).reshape(nodes, ratio, block, block)
    l_sel = jnp.stack(picked_l)

    f32 = jnp.float32
    dma = pltpu.SemaphoreType.DMA
    sends = ratio - 1 + n_cols // 2 - 1 + ratio
    vmem = pl.BlockSpec(memory_space=pltpu.VMEM)
    pieces, diagonal = pl.pallas_call(
        functools.partial(fused, n_rows, n_cols),
        out_shape=(
            jax.ShapeDtypeStruct((nodes, piece, width), jnp.bfloat16),
            jax.ShapeDtypeStruct((nodes, width, width), f32),
        ),
        in_specs=[vmem] * 3,
        out_specs=(vmem, vmem),
        scratch_shapes=[
            pltpu.VMEM((nodes, ratio, block, width), jnp.bfloat16),
            pltpu.VMEM((nodes, n_cols, piece, width), f32),
            pltpu.VMEM((nodes, n_cols, piece, width), f32),
            pltpu.VMEM((nodes, n_cols, piece, width), f32),
            pltpu.VMEM((nodes, n_rows, seg, width), f32),
            pltpu.VMEM((nodes, n_rows, seg, width), f32),
            pltpu.VMEM((nodes, n_cols, seg, width), f32),
            pltpu.VMEM((nodes, n_rows, seg, width), f32),
            dma((nodes, CHUNKS, sends)), dma((nodes, ratio, CHUNKS)),
            dma((nodes, n_cols)), dma((nodes, n_cols)),
            dma((nodes, n_cols)), dma((nodes, n_cols)),
            dma((nodes, n_rows)), dma((nodes, n_rows)),
            dma((nodes, n_cols)), dma((nodes, n_cols)),
            dma((nodes, n_rows)), dma((nodes, n_rows)),
        ],
        compiler_params=pltpu.CompilerParams(
            collective_id=0, has_side_effects=True, vmem_limit_bytes=40 * 1024 * 1024
        ),
        name="selected_inverse",
    )(a_sel, l_sel, diag_inverse)

    local = jnp.arange(rows_local, dtype=jnp.int32)
    mask = jnp.stack(row_picks)[:, None] == local[None, :]
    off_diag = jnp.where(mask[:, :, None, None], pieces[:, None], jnp.zeros((), jnp.bfloat16))
    return off_diag, diagonal


def solution(mesh):
    placed = (P(None, "prow", None, "pcol"), P(None, None, "prow", None), P(), P())
    return jax.shard_map(
        on_device,
        mesh=mesh,
        in_specs=placed,
        out_specs=(P(None, None, ("prow", "pcol"), None), P()),
        check_vma=False,
    )
```

time: 308 us -> 94.2 us (0.31)
  waiting for transfers between devices: 234 us -> 0 us
  Pallas kernels: 0 us -> 64.4 us
  matrix products: 39.9 us -> 0 us
  between operations: 17.8 us -> 12.1 us
  local copies, waits for them, and re-layouts: 8.2 us -> 12.3 us
    psum x1 -> x0, waiting for transfers between devices: 131 us -> none  [on_device(): diagonal_terms = lax.psum(jnp.stack(products), ('prow', 'pcol'))]
    reduce_scatter x2 -> x0, waiting for transfers between devices: 67.9 us -> none  [on_device(): lax.psum_scatter(partial_value, 'pcol', scatter_dimension=1, tiled=True)]
    pallas_call x0 -> x1, Pallas kernels: none -> 64.4 us  [on_device(): pl.pallas_call(functools.partial(fused, n_rows, n_cols), out_shape=(jax.S...]
    dot_general x4 -> x0, matrix products: 39.9 us -> none  [the longest x2 37.1 us: on_device(): jnp.einsum('racb,cbw->raw', inverse, column_panel, preferred_element_type...]
    all_gather x2 -> x0, waiting for transfers between devices: 35.1 us -> none  [on_device(): gathered = lax.all_gather(single, 'prow', axis=0, tiled=True)]
    dynamic_slice x4 -> x1, local copies, waits for them, and re-layouts: 1.83 us -> 9.82 us  [on_device(): lax.dynamic_slice(inverse, (row, 0, col, 0), (1, block, 1, block))]
    mul x2 -> x0, other arithmetic: 3.15 us -> none  [on_device(): column_panel = tiled * own_cols.astype(jnp.bfloat16)[:, None, None]]
  transfers between devices with their start and end apart: 5 -> 0, of which waited for: 5 -> 0; matrix products, arithmetic and copies ran while one was open for 15% -> 0% of each run, Pallas kernels for 0% -> 0%
where the time goes in v1:
time: 94.2 us; the launch traced here: 93.8 us
  Pallas kernels  64.4 us (68%)
  local copies, waits for them, and re-layouts  12.3 us (13%)
  between operations  12.1 us (13%)
  other arithmetic  4.94 us (5%)
    pallas_call x1, Pallas kernels, on_device(): pl.pallas_call(functools.partial(fused, n_rows, n_cols), out_shape=(jax.S...  64.4 us
    dynamic_slice x1, local copies, waits for them, and re-layouts, on_device(): lax.dynamic_slice(inverse, (row, 0, col, 0), (1, block, 1, block))  9.82 us

profile of v1, /device:TPU:0, one launch (start us, length us, event | category | flops | bytes accessed | tf_op | source)
XLA Modules:
  0.0 93.8 jit_solution(16770681715970230153)
XLA Ops:
  0.6 0.8 and_select_fusion.3
  1.4 1.5 %fusion.2 = (s32[]{:T(128)}, s32[]{:T(128)}, s32[]{:T(128)}, s32[]{:T(128)}, s32[]{:T(128)}, /*index=5*/s32[]{:T(128)}) fusion(s32[8]{0:T(128)S(1)} %get-tuple-element.26, s32[8]{0:T(128)S(1)} %get-tuple-element.27, s32[]{:T(128)S(6)} %axis_index.25, s32[]{:T(128)S(6)} %add.52, s32[8]{0:T(128)S(1)} %get-tuple-element.25, s32[8]{0:T(128)S(1)} %get-tuple-element.24, ...), kind=kLoop, calls=%fused_computation.38 | loop fusion | flops 378 | bytes 228 | tf_op jit(solution)/shard_map/reduce_sum | solution.py:294
  2.9 1.3 %pad_add_fusion = s32[2]{0:T(128)S(1)} fusion(s32[1]{0:T(128)} %bitcast.3, s32[1]{0:T(128)} %bitcast.1), kind=kLoop, calls=%fused_computation.42 | loop fusion | flops 2 | bytes 16 | tf_op jit(solution)/shard_map/stack | solution.py:336
  4.3 0.1 iota_compare_fusion
  15.8 9.8 %constant_dynamic-slice_fusion.3 = (bf16[1,512,1,512]{3,2,1,0:T(2,128)(2,1)S(1)}, bf16[1,512,1,512]{3,2,1,0:T(2,128)(2,1)S(1)}, bf16[1,512,1,512]{3,2,1,0:T(2,128)(2,1)S(1)}, bf16[1,512,1,512]{3,2,1,0:T(2,128)(2,1)S(1)}) fusion(bf16[4,512,8,512]{3,2,1,0:T(8,128)(2,1)} %param.4, s32[]{:T(128)S(6)} %select_n.86, s32[]{:T(128)S(6)} %select_n.89, ...), kind=kLoop, calls=%fused_computation.24 | loop fusion | bytes 4194328 | tf_op jit(solution)/shard_map/dynamic_slice | solution.py:296
  25.6 0.3 copy_bitcast_fusion
  25.9 0.3 copy_bitcast_fusion.2
  26.2 0.3 pad_maximum_fusion
  26.5 0.0 copy-start
  26.5 1.1 %dynamic-slice_bitcast_fusion.1 = (bf16[1,512,256]{2,1,0:T(8,128)(2,1)S(1)}, bf16[1,512,256]{2,1,0:T(8,128)(2,1)S(1)}) fusion(bf16[2,4,512,256]{3,2,1,0:T(8,128)(2,1)} %param.5, s32[]{:T(128)S(6)} %select_n.86, s32[]{:T(128)S(6)} %select_n.92), kind=kLoop, calls=%fused_computation.8 | loop fusion | bytes 1048584 | tf_op jit(solution)/shard_map/stack;squeeze | solution.py:299
  27.6 0.1 pad_maximum_fusion.1.l_ref
  27.7 0.0 copy-done
  27.7 64.4 %selected_inverse.1 = (bf16[2,128,256]{2,1,0:T(8,128)(2,1)S(1)}, f32[2,256,256]{2,1,0:T(8,128)S(1)}) custom-call(bf16[2,2,512,512]{3,2,1,0:T(8,128)(2,1)S(1)} %bitcast.67, bf16[2,512,256]{2,1,0:T(8,128)(2,1)S(1)} %pad_maximum_fusion.1.l_ref, f32[2,256,256]{2,1,0:T(8,128)S(1)} %copy-done), custom_call_target="tpu_custom_call" | custom-call | tf_op jit(solution)/shard_map/selected_inverse/pallas_call | solution.py:305
  92.1 0.9 broadcast_select_fusion
  93.0 0.8 copy.19
Async XLA Ops:
  26.5 1.2 %copy-start = (f32[2,256,256]{2,1,0:T(8,128)S(1)}, f32[2,256,256]{2,1,0:T(8,128)}, u32[]{:S(2)}) copy-start(f32[2,256,256]{2,1,0:T(8,128)} %d_ref.1) | copy-start | bytes 1572868

commit v2 on v1

--- a/solution.py
+++ b/solution.py
@@ -9,6 +9,7 @@
 
 MESH = pl.DeviceIdType.MESH
 CHUNKS = 2
+STRIPS = 4
 
 
 def remote(src, dst, send, recv, p, q):
@@ -271,37 +272,89 @@
             gath_copy(s, k).wait_send()
 
 
+def pick(
+    n_rows, n_cols, structure_ref, inverse_ref, panel_ref, a_ref, l_ref, mask_ref, raw, wide, a_sem, l_sem
+):
+    p = lax.axis_index("prow")
+    q = lax.axis_index("pcol")
+    nodes, ratio, block, _ = a_ref.shape
+    _, strips, strip, cols_local, _ = raw.shape
+    rows_local = inverse_ref.shape[0]
+    listed = structure_ref.shape[1]
+
+    def find(s, residue, divisor):
+        found = jnp.int32(0)
+        for i in range(listed):
+            value = structure_ref[s, i]
+            found = found + jnp.where(value % n_rows == residue, value // divisor, 0)
+        return found
+
+    copies = []
+    for s in range(nodes):
+        row = find(s, p, n_rows)
+        factor = pltpu.make_async_copy(panel_ref.at[s, row], l_ref.at[s], l_sem.at[s])
+        factor.start()
+        copies.append(factor)
+        for k in range(strips):
+            pltpu.make_async_copy(
+                inverse_ref.at[row, pl.ds(k * strip, strip)], raw.at[s, k], a_sem.at[s, k]
+            ).start()
+        for r in range(rows_local):
+            mask_ref[s, r] = jnp.where(row == r, 1, 0).astype(jnp.int32)
+    for s in range(nodes):
+        cols = [find(s, h * n_cols + q, n_cols) for h in range(ratio)]
+        for k in range(strips):
+            pltpu.make_async_copy(
+                inverse_ref.at[0, pl.ds(k * strip, strip)], raw.at[s, k], a_sem.at[s, k]
+            ).wait()
+            slot = k % 2
+            for b in range(block // 128):
+                lanes = raw[s, k, :, :, b * 128:(b + 1) * 128].astype(jnp.float32)
+                wide[slot, b] = lanes.reshape(strip * cols_local, 128)
+            for h in range(ratio):
+                for b in range(block // 128):
+                    a_ref[s, h, k * strip:(k + 1) * strip, b * 128:(b + 1) * 128] = wide[
+                        slot, b, pl.ds(cols[h], strip, stride=cols_local)
+                    ].astype(jnp.bfloat16)
+    for factor in copies:
+        factor.wait()
+
+
 def on_device(inverse, panel, structure, diag_inverse):
     n_rows = lax.axis_size("prow")
     n_cols = lax.axis_size("pcol")
-    p = lax.axis_index("prow")
-    q = lax.axis_index("pcol")
     rows_local, block, cols_local, _ = inverse.shape
     nodes, _, _, width = panel.shape
     ratio = n_rows // n_cols
     piece = block // n_cols
     seg = width // n_rows
-
-    picked_a = []
-    picked_l = []
-    row_picks = []
-    for s in range(nodes):
-        chosen = structure[s]
-        row = jnp.sum(jnp.where(chosen % n_rows == p, chosen // n_rows, 0))
-        row_picks.append(row)
-        picked_l.append(lax.dynamic_slice(panel, (s, row, 0, 0), (1, 1, block, width))[0, 0])
-        for h in range(ratio):
-            col = jnp.sum(jnp.where(chosen % n_rows == h * n_cols + q, chosen // n_cols, 0))
-            picked_a.append(
-                lax.dynamic_slice(inverse, (row, 0, col, 0), (1, block, 1, block))[0, :, 0, :]
-            )
-    a_sel = jnp.stack(picked_a).reshape(nodes, ratio, block, block)
-    l_sel = jnp.stack(picked_l)
+    strip = block // STRIPS
+
+    vmem = pl.BlockSpec(memory_space=pltpu.VMEM)
+    smem = pl.BlockSpec(memory_space=pltpu.SMEM)
+    hbm = pl.BlockSpec(memory_space=pltpu.HBM)
+    a_sel, l_sel, mask = pl.pallas_call(
+        functools.partial(pick, n_rows, n_cols),
+        out_shape=(
+            jax.ShapeDtypeStruct((nodes, ratio, block, block), jnp.bfloat16),
+            jax.ShapeDtypeStruct((nodes, block, width), jnp.bfloat16),
+            jax.ShapeDtypeStruct((nodes, rows_local), jnp.int32),
+        ),
+        in_specs=[smem, hbm, hbm],
+        out_specs=(vmem, vmem, smem),
+        scratch_shapes=[
+            pltpu.VMEM((nodes, STRIPS, strip, cols_local, block), jnp.bfloat16),
+            pltpu.VMEM((2, block // 128, strip * cols_local, 128), jnp.float32),
+            pltpu.SemaphoreType.DMA((nodes, STRIPS)),
+            pltpu.SemaphoreType.DMA((nodes,)),
+        ],
+        compiler_params=pltpu.CompilerParams(vmem_limit_bytes=50 * 1024 * 1024),
+        name="pick_blocks",
+    )(structure, inverse, panel)
 
     f32 = jnp.float32
     dma = pltpu.SemaphoreType.DMA
     sends = ratio - 1 + n_cols // 2 - 1 + ratio
-    vmem = pl.BlockSpec(memory_space=pltpu.VMEM)
     pieces, diagonal = pl.pallas_call(
         functools.partial(fused, n_rows, n_cols),
         out_shape=(
@@ -332,9 +385,7 @@
         name="selected_inverse",
     )(a_sel, l_sel, diag_inverse)
 
-    local = jnp.arange(rows_local, dtype=jnp.int32)
-    mask = jnp.stack(row_picks)[:, None] == local[None, :]
-    off_diag = jnp.where(mask[:, :, None, None], pieces[:, None], jnp.zeros((), jnp.bfloat16))
+    off_diag = jnp.where(mask[:, :, None, None] > 0, pieces[:, None], jnp.zeros((), jnp.bfloat16))
     return off_diag, diagonal
 
 

time: 94.2 us -> 72.7 us (0.77)
  between operations: 12.1 us -> 0.68 us
  local copies, waits for them, and re-layouts: 12.3 us -> 1.53 us
  Pallas kernels: 64.4 us -> 69.2 us
  other arithmetic: 4.94 us -> 0.91 us
    dynamic_slice x1 -> x0, local copies, waits for them, and re-layouts: 9.82 us -> none  [on_device(): lax.dynamic_slice(inverse, (row, 0, col, 0), (1, block, 1, block))]
    pallas_call x0 -> x1, Pallas kernels: none -> 5.15 us  [on_device(): pl.pallas_call(functools.partial(pick, n_rows, n_cols), out_shape=(jax.Sh...]
    another operation x3 -> x0, local copies, waits for them, and re-layouts: 1.7 us -> none  [the longest x1 1.13 us: on_device(): l_sel = jnp.stack(picked_l)]
    another operation x3 -> x0, other arithmetic: 1.65 us -> none  [the longest x1 1.34 us: on_device(): mask = jnp.stack(row_picks)[:, None] == local[None, :]]
    reduce_sum x1 -> x0, other arithmetic: 1.54 us -> none  [on_device(): jnp.sum(jnp.where(chosen % n_rows == h * n_cols + q, chosen // n_cols, 0))]
where the time goes in v2:
time: 72.7 us; the launch traced here: 72.4 us
  Pallas kernels  69.2 us (95%)
  local copies, waits for them, and re-layouts  1.53 us (2%)
  other arithmetic  0.91 us (1%)
    pallas_call x1, Pallas kernels, on_device(): pl.pallas_call(functools.partial(fused, n_rows, n_cols), out_shape=(jax.S...  64.1 us
    pallas_call x1, Pallas kernels, on_device(): pl.pallas_call(functools.partial(pick, n_rows, n_cols), out_shape=(jax.Sh...  5.15 us
    unnamed x5, local copies, waits for them, and re-layouts  1.53 us

profile of v2, /device:TPU:0, one launch (start us, length us, event | category | flops | bytes accessed | tf_op | source)
XLA Modules:
  0.0 72.4 jit_solution(13841869976667298939)
XLA Ops:
  0.6 0.0 copy-start
  0.6 0.0 copy-start.1
  0.7 0.7 %copy-done.1 = s32[2,8]{1,0:T(2,128)S(1)} copy-done((s32[2,8]{1,0:T(2,128)S(1)}, s32[2,8]{1,0:T(2,128)}, u32[]{:S(2)}) %copy-start.1) | copy-done | bytes 88
  1.4 5.2 %pick_blocks.1 = (bf16[2,2,512,512]{3,2,1,0:T(8,128)(2,1)S(1)}, bf16[2,512,256]{2,1,0:T(8,128)(2,1)S(1)}, s32[2,4]{1,0:T(2,128)S(1)}) custom-call(s32[2,8]{1,0:T(2,128)S(1)} %copy-done.1, bf16[4,512,8,512]{3,2,1,0:T(8,128)(2,1)} %inverse_ref.1, bf16[2,4,512,256]{3,2,1,0:T(8,128)(2,1)} %panel_ref.1), custom_call_target="tpu_custom_call" | custom-call | tf_op jit(solution)/shard_map/pick_blocks/pallas_call | solution.py:336
  6.5 0.0 copy-done
  6.6 64.1 %selected_inverse.1 = (bf16[2,128,256]{2,1,0:T(8,128)(2,1)S(1)}, f32[2,256,256]{2,1,0:T(8,128)S(1)}) custom-call(bf16[2,2,512,512]{3,2,1,0:T(8,128)(2,1)S(1)} %get-tuple-element.8.a_ref, bf16[2,512,256]{2,1,0:T(8,128)(2,1)S(1)} %get-tuple-element.9.l_ref, f32[2,256,256]{2,1,0:T(8,128)S(1)} %copy-done), custom_call_target="tpu_custom_call" | custom-call | tf_op jit(solution)/shard_map/selected_inverse/pallas_call | solution.py:358
  70.7 0.9 %broadcast_select_fusion = bf16[2,4,128,256]{3,2,1,0:T(8,128)(2,1)} fusion(pred[2,4]{1,0:T(4,128)(4,1)S(1)} %broadcast_compare_fusion, bf16[2,128,256]{2,1,0:T(8,128)(2,1)S(1)} %get-tuple-element.10), kind=kLoop, calls=%fused_computation | loop fusion | flops 262144 | bytes 655368 | tf_op jit(solution)/shard_map/jit(_where)/select_n | solution.py:388
  71.6 0.8 %copy.7 = f32[2,256,256]{2,1,0:T(8,128)} copy(f32[2,256,256]{2,1,0:T(8,128)S(1)} %get-tuple-element.15) | data formatting | bytes 1048576
  (1 shorter events, 0.0 us)
Async XLA Ops:
  0.6 5.9 %copy-start = (f32[2,256,256]{2,1,0:T(8,128)S(1)}, f32[2,256,256]{2,1,0:T(8,128)}, u32[]{:S(2)}) copy-start(f32[2,256,256]{2,1,0:T(8,128)} %d_ref.1) | copy-start | bytes 1572868
  0.6 0.7 %copy-start.1 = (s32[2,8]{1,0:T(2,128)S(1)}, s32[2,8]{1,0:T(2,128)}, u32[]{:S(2)}) copy-start(s32[2,8]{1,0:T(2,128)} %structure_ref.1) | copy-start | bytes 196

commit v3 on v2

--- a/solution.py
+++ b/solution.py
@@ -8,7 +8,7 @@
 from jax.sharding import PartitionSpec as P
 
 MESH = pl.DeviceIdType.MESH
-CHUNKS = 2
+SUB = 2
 STRIPS = 4
 
 
@@ -28,7 +28,7 @@
     nodes, ratio, block, width = l_buf.shape
     piece = block // n_cols
     seg = width // n_rows
-    chunk = block // CHUNKS
+    chunk = block // (2 * SUB)
     hi = p // n_cols
     lo = p % n_cols
     t = jnp.int32(0)
@@ -38,11 +38,11 @@
         bit *= 2
     pair = p + 1 - 2 * (p % 2)
 
-    def same_hi(t2):
+    def beside(j):
         lo2 = jnp.int32(0)
         b = 1
         while b < n_cols:
-            lo2 = lo2 + b * (((t2 // b) + (q // b)) % 2)
+            lo2 = lo2 + b * (((lo // b) + (2 * j // b)) % 2)
             b *= 2
         return hi * n_cols + lo2
 
@@ -54,7 +54,7 @@
     pl.semaphore_wait(barrier, n_rows + n_cols - 2)
 
     def rows(c):
-        return pl.ds(c * chunk, chunk)
+        return pl.ds(pl.multiple_of(c * chunk, chunk), chunk)
 
     def l_slot(s, h, c):
         return l_buf.at[s, h, rows(c)]
@@ -65,7 +65,7 @@
 
     def to_x(s, c, j, src):
         return remote(src, l_slot(s, hi, c), l_send.at[s, c, ratio - 1 + j - 1], l_recv.at[s, hi, c],
-                      same_hi(2 * j), q)
+                      beside(j), q)
 
     def to_pair(s, c, k, src):
         h = (hi + k) % ratio
@@ -76,54 +76,86 @@
         remote(l_slot(s, h, c), l_slot(s, h, c), l_send.at[s, c, 0], l_recv.at[s, h, c], pair, q).wait_recv()
 
     owner = t == 0
-    even = t % 2 == 0
+    source_chip = t < 2
+    core = p % 2
+
+    def mine(u):
+        return core * SUB + u
+
+    def other(u):
+        return (1 - core) * SUB + u
 
     @pl.when(owner)
     def _():
         for s in range(nodes):
-            for c in range(CHUNKS):
-                src = l_ref.at[s, rows(c)]
+            for u in range(SUB):
+                to_pair(s, other(u), 0, l_ref.at[s, rows(other(u))]).start()
+            for u in range(SUB):
+                src = l_ref.at[s, rows(mine(u))]
+                for j in range(1, n_cols // 2):
+                    to_x(s, mine(u), j, src).start()
+                for k in range(1, ratio):
+                    to_peer_hi(s, mine(u), k, src).start()
+            for u in range(SUB):
+                to_pair(s, mine(u), 0, l_ref.at[s, rows(mine(u))]).start()
+        for s in range(nodes):
+            l_buf[s, hi] = l_ref[s]
+
+    def receive_blocks(s):
+        for u in range(SUB):
+            c = mine(u)
+            src = l_slot(s, hi, c)
+
+            @pl.when(jnp.logical_not(owner))
+            def _():
+                l_arrived(s, c, hi)
+                for k in range(1, ratio):
+                    to_peer_hi(s, c, k, src).start()
+
+            @pl.when(t == 1)
+            def _():
                 for j in range(1, n_cols // 2):
                     to_x(s, c, j, src).start()
-                for k in range(1, ratio):
-                    to_peer_hi(s, c, k, src).start()
+
+            @pl.when(jnp.logical_not(source_chip))
+            def _():
                 to_pair(s, c, 0, src).start()
-        for s in range(nodes):
-            l_buf[s, hi] = l_ref[s]
-
-    def receive_blocks(s):
-        for c in range(CHUNKS):
-            @pl.when(jnp.logical_not(owner))
-            def _():
-                l_arrived(s, c, hi)
-
-            @pl.when(jnp.logical_and(even, jnp.logical_not(owner)))
-            def _():
-                for k in range(1, ratio):
-                    to_peer_hi(s, c, k, l_slot(s, hi, c)).start()
-                to_pair(s, c, 0, l_slot(s, hi, c)).start()
-
+
+        for u in range(SUB):
+            c = mine(u)
             for k in range(1, ratio):
                 l_arrived(s, c, (hi + k) % ratio)
-
-                @pl.when(even)
-                def _():
-                    to_pair(s, c, k, l_slot(s, (hi + k) % ratio, c)).start()
+                to_pair(s, c, k, l_slot(s, (hi + k) % ratio, c)).start()
+        for u in range(SUB):
+            c = other(u)
+
+            @pl.when(jnp.logical_not(owner))
+            def _():
+                l_arrived(s, c, hi)
+
+            for k in range(1, ratio):
+                l_arrived(s, c, (hi + k) % ratio)
 
     def drain_blocks(s):
-        for c in range(CHUNKS):
-            @pl.when(even)
-            def _():
-                src = l_slot(s, hi, c)
-                for k in range(1, ratio):
-                    to_peer_hi(s, c, k, src).wait_send()
-                for k in range(ratio):
-                    to_pair(s, c, k, src).wait_send()
+        for u in range(SUB):
+            c = mine(u)
+            src = l_slot(s, hi, c)
+            for k in range(1, ratio):
+                to_peer_hi(s, c, k, src).wait_send()
+                to_pair(s, c, k, src).wait_send()
+
+            @pl.when(source_chip)
+            def _():
+                for j in range(1, n_cols // 2):
+                    to_x(s, c, j, src).wait_send()
+
+            @pl.when(t != 1)
+            def _():
+                to_pair(s, c, 0, src).wait_send()
 
             @pl.when(owner)
             def _():
-                for j in range(1, n_cols // 2):
-                    to_x(s, c, j, l_slot(s, hi, c)).wait_send()
+                to_pair(s, other(u), 0, src).wait_send()
 
     def multiply(s):
         total = jnp.dot(a_ref[s, 0], l_buf[s, 0], preferred_element_type=jnp.float32)
@@ -131,6 +163,16 @@
             total += jnp.dot(a_ref[s, h], l_buf[s, h], preferred_element_type=jnp.float32)
         for d in range(n_cols):
             part[s, d] = total[d * piece:(d + 1) * piece]
+        return total
+
+    def diagonal_term(s, total):
+        high = total.astype(jnp.bfloat16)
+        low = (total - high.astype(jnp.float32)).astype(jnp.bfloat16)
+        over_rows = (((0,), (0,)), ((), ()))
+        product = lax.dot_general(l_ref[s], high, over_rows, preferred_element_type=jnp.float32)
+        product += lax.dot_general(l_ref[s], low, over_rows, preferred_element_type=jnp.float32)
+        for k in range(n_rows):
+            term[s, k] = product[k * seg:(k + 1) * seg]
 
     def right_copy(s, d, src):
         return remote(src, right_buf.at[s, d], r_send.at[s, d], r_recv.at[s, d], p, (q + 1) % n_cols)
@@ -138,15 +180,15 @@
     def left_copy(s, d, src):
         return remote(src, left_buf.at[s, d], f_send.at[s, d], f_recv.at[s, d], p, (q + n_cols - 1) % n_cols)
 
-    def line_start(s):
+    def line_start(s, nearest):
         @pl.when(q == 0)
         def _():
-            for d in range(n_cols - 1, 0, -1):
+            for d in ((1,) if nearest else range(n_cols - 1, 1, -1)):
                 right_copy(s, d, part.at[s, d]).start()
 
         @pl.when(q == n_cols - 1)
         def _():
-            for d in range(n_cols - 1):
+            for d in ((n_cols - 2,) if nearest else range(n_cols - 2)):
                 left_copy(s, d, part.at[s, d]).start()
 
     def line_relay(s):
@@ -178,14 +220,7 @@
             left_copy(s, q, left_buf.at[s, q]).wait_recv()
             part[s, q] = part[s, q] + left_buf[s, q]
 
-        rounded = (-part[s, q]).astype(jnp.bfloat16)
-        y_ref[s] = rounded
-        factor = l_ref[s, pl.ds(pl.multiple_of(q * piece, piece), piece)]
-        product = lax.dot_general(
-            factor, rounded, (((0,), (0,)), ((), ())), preferred_element_type=jnp.float32
-        )
-        for k in range(n_rows):
-            term[s, k] = product[k * seg:(k + 1) * seg]
+        y_ref[s] = (-part[s, q]).astype(jnp.bfloat16)
 
     def line_drain(s):
         for d in range(n_cols):
@@ -239,22 +274,29 @@
         total = col_buf[s, 0]
         for k in range(1, n_cols):
             total = total + col_buf[s, k]
-        gath[s, p] = d_ref[s, pl.ds(pl.multiple_of(p * seg, seg), seg)] - total
+        gath[s, p] = d_ref[s, pl.ds(pl.multiple_of(p * seg, seg), seg)] + total
         for k in range(1, n_rows):
             gath_copy(s, k).start()
 
     for s in range(nodes):
         receive_blocks(s)
-        multiply(s)
-        line_start(s)
+        total = multiply(s)
+        if s > 0:
+            col_start(s - 1)
+            line_start(s - 1, True)
+        line_start(s, False)
+        diagonal_term(s, total)
+        plane_start(s)
     for s in range(nodes):
         line_relay(s)
+        if s == 0:
+            col_start(nodes - 1)
+            line_start(nodes - 1, True)
+        if s < nodes - 1:
+            gath_start(s)
+    gath_start(nodes - 1)
+    for s in range(nodes):
         line_finish(s)
-        plane_start(s)
-    for s in range(nodes):
-        col_start(s)
-    for s in range(nodes):
-        gath_start(s)
     for s in range(nodes):
         drain_blocks(s)
         line_drain(s)
@@ -372,7 +414,7 @@
             pltpu.VMEM((nodes, n_rows, seg, width), f32),
             pltpu.VMEM((nodes, n_cols, seg, width), f32),
             pltpu.VMEM((nodes, n_rows, seg, width), f32),
-            dma((nodes, CHUNKS, sends)), dma((nodes, ratio, CHUNKS)),
+            dma((nodes, 2 * SUB, sends)), dma((nodes, ratio, 2 * SUB)),
             dma((nodes, n_cols)), dma((nodes, n_cols)),
             dma((nodes, n_cols)), dma((nodes, n_cols)),
             dma((nodes, n_rows)), dma((nodes, n_rows)),

time: 72.7 us -> 64.6 us (0.89)
  the two profiles are of different devices: /device:TPU:0 before, /device:TPU:9 now
where the time goes in v3:
time: 64.6 us; the launch traced here: 64.4 us
  Pallas kernels  61.3 us (95%)
  local copies, waits for them, and re-layouts  1.53 us (2%)
  other arithmetic  0.91 us (1%)
  between operations  0.68 us (1%)
    pallas_call x1, Pallas kernels, on_device(): pl.pallas_call(functools.partial(fused, n_rows, n_cols), out_shape=(jax.S...  56.2 us
    pallas_call x1, Pallas kernels, on_device(): pl.pallas_call(functools.partial(pick, n_rows, n_cols), out_shape=(jax.Sh...  5.15 us
    unnamed x5, local copies, waits for them, and re-layouts  1.53 us

profile of v3, /device:TPU:9, one launch (start us, length us, event | category | flops | bytes accessed | tf_op | source)
XLA Modules:
  0.0 64.4 jit_solution(5861993661022276167)
XLA Ops:
  0.6 0.0 copy-start
  0.6 0.0 copy-start.1
  0.7 0.7 %copy-done.1 = s32[2,8]{1,0:T(2,128)S(1)} copy-done((s32[2,8]{1,0:T(2,128)S(1)}, s32[2,8]{1,0:T(2,128)}, u32[]{:S(2)}) %copy-start.1) | copy-done | bytes 88
  1.4 5.2 %pick_blocks.1 = (bf16[2,2,512,512]{3,2,1,0:T(8,128)(2,1)S(1)}, bf16[2,512,256]{2,1,0:T(8,128)(2,1)S(1)}, s32[2,4]{1,0:T(2,128)S(1)}) custom-call(s32[2,8]{1,0:T(2,128)S(1)} %copy-done.1, bf16[4,512,8,512]{3,2,1,0:T(8,128)(2,1)} %inverse_ref.1, bf16[2,4,512,256]{3,2,1,0:T(8,128)(2,1)} %panel_ref.1), custom_call_target="tpu_custom_call" | custom-call | tf_op jit(solution)/shard_map/pick_blocks/pallas_call | solution.py:378
  6.5 0.0 copy-done
  6.6 56.2 %selected_inverse.1 = (bf16[2,128,256]{2,1,0:T(8,128)(2,1)S(1)}, f32[2,256,256]{2,1,0:T(8,128)S(1)}) custom-call(bf16[2,2,512,512]{3,2,1,0:T(8,128)(2,1)S(1)} %get-tuple-element.8.a_ref, bf16[2,512,256]{2,1,0:T(8,128)(2,1)S(1)} %get-tuple-element.9.l_ref, f32[2,256,256]{2,1,0:T(8,128)S(1)} %copy-done), custom_call_target="tpu_custom_call" | custom-call | tf_op jit(solution)/shard_map/selected_inverse/pallas_call | solution.py:400
  62.7 0.9 %broadcast_select_fusion = bf16[2,4,128,256]{3,2,1,0:T(8,128)(2,1)} fusion(pred[2,4]{1,0:T(4,128)(4,1)S(1)} %broadcast_compare_fusion, bf16[2,128,256]{2,1,0:T(8,128)(2,1)S(1)} %get-tuple-element.10), kind=kLoop, calls=%fused_computation | loop fusion | flops 262144 | bytes 655368 | tf_op jit(solution)/shard_map/jit(_where)/select_n | solution.py:430
  63.6 0.8 %copy.7 = f32[2,256,256]{2,1,0:T(8,128)} copy(f32[2,256,256]{2,1,0:T(8,128)S(1)} %get-tuple-element.15) | data formatting | bytes 1048576
  (1 shorter events, 0.0 us)
Async XLA Ops:
  0.6 5.9 %copy-start = (f32[2,256,256]{2,1,0:T(8,128)S(1)}, f32[2,256,256]{2,1,0:T(8,128)}, u32[]{:S(2)}) copy-start(f32[2,256,256]{2,1,0:T(8,128)} %d_ref.1) | copy-start | bytes 1572868
  0.6 0.7 %copy-start.1 = (s32[2,8]{1,0:T(2,128)S(1)}, s32[2,8]{1,0:T(2,128)}, u32[]{:S(2)}) copy-start(s32[2,8]{1,0:T(2,128)} %structure_ref.1) | copy-start | bytes 196

commit v4 on v3

--- a/solution.py
+++ b/solution.py
@@ -20,7 +20,7 @@
 
 def fused(
     n_rows, n_cols, a_ref, l_ref, d_ref, y_ref, g_ref,
-    l_buf, part, right_buf, left_buf, term, plane_buf, col_buf, gath,
+    l_buf, part, right_buf, left_buf, right_scale, left_scale, term, plane_buf, col_buf, gath,
     l_send, l_recv, r_send, r_recv, f_send, f_recv, p_send, p_recv, c_send, c_recv, g_send, g_recv,
 ):
     p = lax.axis_index("prow")
@@ -174,22 +174,51 @@
         for k in range(n_rows):
             term[s, k] = product[k * seg:(k + 1) * seg]
 
-    def right_copy(s, d, src):
-        return remote(src, right_buf.at[s, d], r_send.at[s, d], r_recv.at[s, d], p, (q + 1) % n_cols)
-
-    def left_copy(s, d, src):
-        return remote(src, left_buf.at[s, d], f_send.at[s, d], f_recv.at[s, d], p, (q + n_cols - 1) % n_cols)
+    def encode(s, d, value, buf, scale):
+        largest = jnp.maximum(jnp.max(jnp.abs(value), axis=0, keepdims=True), 1e-30)
+        buf[s, d] = jnp.floor(value * (32700.0 / largest) + 0.5).astype(jnp.int32).astype(jnp.int16)
+        scale[s, d] = jnp.broadcast_to(largest * (1.0 / 32700.0), scale.shape[2:])
+
+    def decode(s, d, buf, scale):
+        return buf[s, d].astype(jnp.int32).astype(jnp.float32) * scale[s, d][0:1]
+
+    class line_copy:
+        def __init__(self, s, d, buf, scale, send, recv, to):
+            self.copies = [
+                remote(buf.at[s, d], buf.at[s, d], send.at[0, s, d], recv.at[0, s, d], p, to),
+                remote(scale.at[s, d], scale.at[s, d], send.at[1, s, d], recv.at[1, s, d], p, to),
+            ]
+
+        def start(self):
+            for copy in self.copies:
+                copy.start()
+
+        def wait_send(self):
+            for copy in self.copies:
+                copy.wait_send()
+
+        def wait_recv(self):
+            for copy in self.copies:
+                copy.wait_recv()
+
+    def right_copy(s, d):
+        return line_copy(s, d, right_buf, right_scale, r_send, r_recv, (q + 1) % n_cols)
+
+    def left_copy(s, d):
+        return line_copy(s, d, left_buf, left_scale, f_send, f_recv, (q + n_cols - 1) % n_cols)
 
     def line_start(s, nearest):
         @pl.when(q == 0)
         def _():
             for d in ((1,) if nearest else range(n_cols - 1, 1, -1)):
-                right_copy(s, d, part.at[s, d]).start()
+                encode(s, d, part[s, d], right_buf, right_scale)
+                right_copy(s, d).start()
 
         @pl.when(q == n_cols - 1)
         def _():
             for d in ((n_cols - 2,) if nearest else range(n_cols - 2)):
-                left_copy(s, d, part.at[s, d]).start()
+                encode(s, d, part[s, d], left_buf, left_scale)
+                left_copy(s, d).start()
 
     def line_relay(s):
         for i in range(n_cols - 2):
@@ -197,28 +226,28 @@
 
             @pl.when(jnp.logical_and(q > 0, q < d))
             def _():
-                right_copy(s, d, right_buf.at[s, d]).wait_recv()
-                right_buf[s, d] = right_buf[s, d] + part[s, d]
-                right_copy(s, d, right_buf.at[s, d]).start()
+                right_copy(s, d).wait_recv()
+                encode(s, d, decode(s, d, right_buf, right_scale) + part[s, d], right_buf, right_scale)
+                right_copy(s, d).start()
 
             e = i
 
             @pl.when(jnp.logical_and(q < n_cols - 1, q > e))
             def _():
-                left_copy(s, e, left_buf.at[s, e]).wait_recv()
-                left_buf[s, e] = left_buf[s, e] + part[s, e]
-                left_copy(s, e, left_buf.at[s, e]).start()
+                left_copy(s, e).wait_recv()
+                encode(s, e, decode(s, e, left_buf, left_scale) + part[s, e], left_buf, left_scale)
+                left_copy(s, e).start()
 
     def line_finish(s):
         @pl.when(q > 0)
         def _():
-            right_copy(s, q, right_buf.at[s, q]).wait_recv()
-            part[s, q] = part[s, q] + right_buf[s, q]
+            right_copy(s, q).wait_recv()
+            part[s, q] = part[s, q] + decode(s, q, right_buf, right_scale)
 
         @pl.when(q < n_cols - 1)
         def _():
-            left_copy(s, q, left_buf.at[s, q]).wait_recv()
-            part[s, q] = part[s, q] + left_buf[s, q]
+            left_copy(s, q).wait_recv()
+            part[s, q] = part[s, q] + decode(s, q, left_buf, left_scale)
 
         y_ref[s] = (-part[s, q]).astype(jnp.bfloat16)
 
@@ -226,11 +255,11 @@
         for d in range(n_cols):
             @pl.when(q < d)
             def _():
-                right_copy(s, d, part.at[s, d]).wait_send()
+                right_copy(s, d).wait_send()
 
             @pl.when(q > d)
             def _():
-                left_copy(s, d, part.at[s, d]).wait_send()
+                left_copy(s, d).wait_send()
 
     def plane_copy(s, k):
         to = (p + k) % n_rows
@@ -408,15 +437,17 @@
         scratch_shapes=[
             pltpu.VMEM((nodes, ratio, block, width), jnp.bfloat16),
             pltpu.VMEM((nodes, n_cols, piece, width), f32),
-            pltpu.VMEM((nodes, n_cols, piece, width), f32),
-            pltpu.VMEM((nodes, n_cols, piece, width), f32),
+            pltpu.VMEM((nodes, n_cols, piece, width), jnp.int16),
+            pltpu.VMEM((nodes, n_cols, piece, width), jnp.int16),
+            pltpu.VMEM((nodes, n_cols, 8, width), f32),
+            pltpu.VMEM((nodes, n_cols, 8, width), f32),
             pltpu.VMEM((nodes, n_rows, seg, width), f32),
             pltpu.VMEM((nodes, n_rows, seg, width), f32),
             pltpu.VMEM((nodes, n_cols, seg, width), f32),
             pltpu.VMEM((nodes, n_rows, seg, width), f32),
             dma((nodes, 2 * SUB, sends)), dma((nodes, ratio, 2 * SUB)),
-            dma((nodes, n_cols)), dma((nodes, n_cols)),
-            dma((nodes, n_cols)), dma((nodes, n_cols)),
+            dma((2, nodes, n_cols)), dma((2, nodes, n_cols)),
+            dma((2, nodes, n_cols)), dma((2, nodes, n_cols)),
             dma((nodes, n_rows)), dma((nodes, n_rows)),
             dma((nodes, n_cols)), dma((nodes, n_cols)),
             dma((nodes, n_rows)), dma((nodes, n_rows)),

time: 64.6 us -> 57 us (0.88); the launches traced: 64.4 us -> 56.1 us
  Pallas kernels: 61.3 us -> 53 us
    pallas_call x1, Pallas kernels: 56.2 us -> 47.8 us  [on_device(): pl.pallas_call(functools.partial(fused, n_rows, n_cols), out_shape=(jax.S...]
where the time goes in v4:
time: 57 us; the launch traced here: 56.1 us
  Pallas kernels  53 us (93%)
  local copies, waits for them, and re-layouts  1.53 us (3%)
  other arithmetic  0.91 us (2%)
  between operations  0.68 us (1%)
    pallas_call x1, Pallas kernels, on_device(): pl.pallas_call(functools.partial(fused, n_rows, n_cols), out_shape=(jax.S...  47.8 us
    pallas_call x1, Pallas kernels, on_device(): pl.pallas_call(functools.partial(pick, n_rows, n_cols), out_shape=(jax.Sh...  5.15 us
    unnamed x5, local copies, waits for them, and re-layouts  1.53 us

profile of v4, /device:TPU:9, one launch (start us, length us, event | category | flops | bytes accessed | tf_op | source)
XLA Modules:
  0.0 56.1 jit_solution(8295043415837479433)
XLA Ops:
  0.6 0.0 copy-start
  0.6 0.0 copy-start.1
  0.7 0.7 %copy-done.1 = s32[2,8]{1,0:T(2,128)S(1)} copy-done((s32[2,8]{1,0:T(2,128)S(1)}, s32[2,8]{1,0:T(2,128)}, u32[]{:S(2)}) %copy-start.1) | copy-done | bytes 88
  1.4 5.2 %pick_blocks.1 = (bf16[2,2,512,512]{3,2,1,0:T(8,128)(2,1)S(1)}, bf16[2,512,256]{2,1,0:T(8,128)(2,1)S(1)}, s32[2,4]{1,0:T(2,128)S(1)}) custom-call(s32[2,8]{1,0:T(2,128)S(1)} %copy-done.1, bf16[4,512,8,512]{3,2,1,0:T(8,128)(2,1)} %inverse_ref.1, bf16[2,4,512,256]{3,2,1,0:T(8,128)(2,1)} %panel_ref.1), custom_call_target="tpu_custom_call" | custom-call | tf_op jit(solution)/shard_map/pick_blocks/pallas_call | solution.py:407
  6.5 0.0 copy-done
  6.6 47.8 %selected_inverse.1 = (bf16[2,128,256]{2,1,0:T(8,128)(2,1)S(1)}, f32[2,256,256]{2,1,0:T(8,128)S(1)}) custom-call(bf16[2,2,512,512]{3,2,1,0:T(8,128)(2,1)S(1)} %get-tuple-element.8.a_ref, bf16[2,512,256]{2,1,0:T(8,128)(2,1)S(1)} %get-tuple-element.9.l_ref, f32[2,256,256]{2,1,0:T(8,128)S(1)} %copy-done), custom_call_target="tpu_custom_call" | custom-call | tf_op jit(solution)/shard_map/selected_inverse/pallas_call | solution.py:429
  54.4 0.9 %broadcast_select_fusion = bf16[2,4,128,256]{3,2,1,0:T(8,128)(2,1)} fusion(pred[2,4]{1,0:T(4,128)(4,1)S(1)} %broadcast_compare_fusion, bf16[2,128,256]{2,1,0:T(8,128)(2,1)S(1)} %get-tuple-element.10), kind=kLoop, calls=%fused_computation | loop fusion | flops 262144 | bytes 655368 | tf_op jit(solution)/shard_map/jit(_where)/select_n | solution.py:461
  55.3 0.8 %copy.7 = f32[2,256,256]{2,1,0:T(8,128)} copy(f32[2,256,256]{2,1,0:T(8,128)S(1)} %get-tuple-element.15) | data formatting | bytes 1048576
  (1 shorter events, 0.0 us)
Async XLA Ops:
  0.6 5.9 %copy-start = (f32[2,256,256]{2,1,0:T(8,128)S(1)}, f32[2,256,256]{2,1,0:T(8,128)}, u32[]{:S(2)}) copy-start(f32[2,256,256]{2,1,0:T(8,128)} %d_ref.1) | copy-start | bytes 1572868
  0.6 0.7 %copy-start.1 = (s32[2,8]{1,0:T(2,128)S(1)}, s32[2,8]{1,0:T(2,128)}, u32[]{:S(2)}) copy-start(s32[2,8]{1,0:T(2,128)} %structure_ref.1) | copy-start | bytes 196
